TPU v7x, 512 devices: a whole 4x4x16 slice. The times are simulated.
512 devices in a mesh: row: 16 (over z), col: 32 (over y, x, core).
Axes of the slice: x: 4, y: 4, z: 16, core: 2. Of those that a mesh axis runs over, the one named last changes fastest.
Arguments:
- tokens: bfloat16 [2048, 8192], P('row'), may hold values from -6 to 6
- gate_weight: bfloat16 [8192, 16384], P('row', 'col'), may hold values from -0.09375 to 0.09375
- up_weight: bfloat16 [8192, 16384], P('row', 'col'), may hold values from -0.09375 to 0.09375
- down_weight: bfloat16 [16384, 8192], P('col', 'row'), may hold values from -0.0625 to 0.0625
- gate_mask: int32 [64, 128], P('row', 'col'), may hold values from 0 to 1, as said below
- up_mask: int32 [64, 128], P('row', 'col'), may hold values from 0 to 1, as said below
- down_mask: int32 [128, 64], P('col', 'row'), may hold values 0 or 1
Outputs:
- mixed: bfloat16 [2048, 8192], P('col', 'row')
Inputs may be any that keep to these rules, and one draw needn't show every extreme that they name: `gate_mask`: each device's block of 4 x 4 tiles keeps between 4 and 12 tiles; in each column of devices some block keeps exactly 12. `up_mask`: as for gate_mask, drawn independently.
All inputs are finite; a program needn't handle non-finite values. No bound on the sum of `down_mask` on one device may be relied on, other than what follows from the above.
Results may differ from a plain program's by a relative error of at most 0.02.
Values may be sent and summed in bfloat16 or wider, within the bound.
A program may use at most 128 MiB of HBM per device.

v0:
```python
import jax
import jax.numpy as jnp
from jax import lax
from jax.sharding import PartitionSpec as P


def expand(weight, mask):
    rows, cols = weight.shape
    tile_rows, tile_cols = mask.shape
    tile = rows // tile_rows
    shaped = weight.reshape(tile_rows, tile, tile_cols, tile)
    return (shaped * mask.astype(weight.dtype)[:, None, :, None]).reshape(rows, cols)


def pack_tiles(weight, mask):
    rows, cols = weight.shape
    tile_rows, tile_cols = mask.shape
    tile = rows // tile_rows
    count = tile_rows * tile_cols
    slots = 3 * count // 4
    tiles = (
        weight.reshape(tile_rows, tile, tile_cols, tile)
        .transpose(0, 2, 1, 3)
        .reshape(count, tile * tile)
    )
    flags = mask.reshape(count)
    place = jnp.cumsum(flags) - 1
    chosen = (place[None, :] == jnp.arange(slots, dtype=jnp.int32)[:, None]) & (flags[None, :] == 1)
    packed = jnp.dot(chosen.astype(jnp.bfloat16), tiles, preferred_element_type=jnp.float32)
    packed = packed.astype(jnp.bfloat16).reshape(slots, tile, tile)
    where_from = jnp.sum(jnp.where(chosen, jnp.arange(count, dtype=jnp.int32)[None, :], 0), axis=1)
    return (packed, where_from)


def unpack_tiles(packed, where_from, groups, tile_rows, tile_cols):
    slots, tile = (packed.shape[0] // groups, packed.shape[1])
    count = tile_rows * tile_cols
    packed = packed.reshape(groups, slots, tile, tile)
    where_from = where_from.reshape(groups, slots)
    spread = (where_from[:, None, :] == jnp.arange(count, dtype=jnp.int32)[None, :, None]).astype(
        jnp.bfloat16
    )
    dense = jnp.einsum("gcs,gsab->gcab", spread, packed, preferred_element_type=jnp.float32).astype(
        jnp.bfloat16
    )
    dense = dense.reshape(groups, tile_rows, tile_cols, tile, tile).transpose(0, 1, 3, 2, 4)
    return dense.reshape(groups, tile_rows * tile, tile_cols * tile)


def on_device(tokens, gate_weight, up_weight, down_weight, gate_mask, up_mask, down_mask):
    tok_rows = tokens.shape[0]
    panel_rows, panel_cols = gate_weight.shape
    tile_rows, tile_cols = gate_mask.shape
    slots = 3 * tile_rows * tile_cols // 4
    gate_packed, gate_from = pack_tiles(gate_weight, gate_mask)
    up_packed, up_from = pack_tiles(up_weight, up_mask)
    gate_piece = lax.all_gather(gate_packed, "row", axis=0, tiled=True)
    up_piece = lax.all_gather(up_packed, "row", axis=0, tiled=True)
    gate_where = lax.all_gather(gate_from, "row", axis=0, tiled=True)
    up_where = lax.all_gather(up_from, "row", axis=0, tiled=True)
    groups = gate_piece.shape[0] // slots
    columns = tokens
    columns = columns.reshape(tok_rows, groups, panel_rows)

    def partial_value(piece, where_from):
        dense = unpack_tiles(piece, where_from, groups, tile_rows, tile_cols)
        product = jnp.einsum("tgr,grc->gtc", columns, dense, preferred_element_type=jnp.float32)
        rounded = lax.optimization_barrier(product.astype(jnp.bfloat16)).astype(jnp.float32)
        return jnp.sum(rounded, axis=0)

    gate = partial_value(gate_piece, gate_where)
    up = partial_value(up_piece, up_where)
    hidden = (jax.nn.silu(gate) * up).astype(jnp.bfloat16)
    all_hidden = lax.all_gather(hidden, "row", axis=0, tiled=True)
    down_eff = expand(down_weight, down_mask)
    return lax.psum_scatter(
        jnp.dot(all_hidden, down_eff, preferred_element_type=jnp.float32).astype(jnp.bfloat16),
        "col",
        scatter_dimension=0,
        tiled=True,
    )


def solution(mesh):
    return jax.shard_map(
        on_device,
        mesh=mesh,
        in_specs=(
            P("row", None),
            P("row", "col"),
            P("row", "col"),
            P("col", "row"),
            P("row", "col"),
            P("row", "col"),
            P("col", "row"),
        ),
        out_specs=P("col", "row"),
        check_vma=False,
    )
```

profile of v0, /device:TPU:1, one launch (start us, length us, event | category | flops | bytes accessed | tf_op | source)
XLA Modules:
  0.0 405.0 jit_solution(13095400725307765612)
XLA Ops:
  6.5 0.0 all-gather.4.cloned.1.call-start
  6.5 0.8 reshape.148
  7.3 0.7 broadcast_compare_fusion.1
  8.0 0.1 add_reduce_fusion.1
  8.1 0.1 eq.82
  8.2 1.2 reshape.122
  9.4 0.1 copy.33
  9.5 0.4 convolution_convert_fusion.1
  9.9 0.1 copy.48
  10.0 0.8 slice
  10.8 0.0 all-gather.4.cloned.1.call-update
  10.8 0.0 all-gather.6.cloned.1.call-start
  10.9 0.8 reshape.149
  11.6 0.7 broadcast_compare_fusion
  12.3 0.1 eq.91
  12.4 1.2 reshape.130
  13.6 0.1 copy.38
  13.7 0.1 add_reduce_fusion
  13.8 0.4 convolution_convert_fusion
  14.3 0.1 copy.50
  14.4 0.8 slice.1
  15.2 0.0 all-gather.6.cloned.1.call-update
  15.2 0.0 all-gather.8.cloned.1.call-start
  15.2 1.3 dynamic-slice
  17.2 0.1 select_reduce_fusion.1
  17.3 0.2 dynamic-update-slice
  17.5 0.1 select_reduce_fusion
  17.6 0.2 dynamic-update-slice.1
  17.9 23.9 %all-reduce.2 = (s32[192]{0:T(256)S(1)}, s32[192]{0:T(256)S(1)}) all-reduce(s32[192]{0:T(256)S(1)} %dynamic-update-slice.1, s32[192]{0:T(256)S(1)} %dynamic-update-slice), channel_id=1, replica_groups=mesh['row'=16,'col'=32] {'row'}, use_global_device_ids=true, to_apply=%add.1 | all-reduce | flops 384 | bytes 3072
  41.8 0.1 eq.83
  41.9 0.1 eq.92
  42.0 58.8 %all-gather.4.cloned.1.call-done = bf16[192,128,128]{2,1,0:T(8,128)(2,1)} async-done(((bf16[12,128,128]{2,1,0:T(8,128)(2,1)}), bf16[192,128,128]{2,1,0:T(8,128)(2,1)}) %all-gather.4.cloned.1.call-update) | async-done | bytes 6291472 | tf_op jit(solution)/shard_map/all_gather | solution.py:57
  100.8 10.4 %fusion.4 = bf16[16,16,128,128]{3,1,2,0:T(8,128)(2,1)} fusion(bf16[16,12,128,128]{3,2,1,0:T(8,128)(2,1)} %bitcast.65, s32[16,12]{1,0:T(8,128)S(1)} %eq.83), kind=kOutput, calls=%fused_computation.7 | convolution fusion | flops 104860672 | bytes 14680832 | tf_op jit(solution)/shard_map/gcs,gsab->gcab/dot_general | solution.py:43
  111.2 15.4 %copy.35 = bf16[16,4,128,4,128]{2,1,4,3,0:T(4,128)(2,1)} copy(bf16[16,4,128,4,128]{4,3,1,2,0:T(4,128)(2,1)} %bitcast.62) | data formatting | bytes 16777216 | tf_op jit(solution)/shard_map/transpose | solution.py:46
  126.5 13.2 %reshape.127 = bf16[16,512,512]{1,2,0:T(8,128)(2,1)} reshape(bf16[16,4,128,4,128]{2,1,4,3,0:T(4,128)(2,1)} %copy.35) | data formatting | bytes 16777216 | tf_op jit(solution)/shard_map/reshape | solution.py:47
  139.7 6.4 %convert_bitcast_fusion.1 = bf16[16,128,512]{1,2,0:T(8,128)(2,1)S(1)} fusion(bf16[16,512,512]{1,2,0:T(8,128)(2,1)} %reshape.127, bf16[16,16,8,512]{3,2,1,0:T(8,128)(2,1)} %bitcast.74), kind=kOutput, calls=%fused_computation.17 | convolution fusion | flops 1074790400 | bytes 12582912 | tf_op jit(solution)/shard_map/tgr,grc->gtc/dot_general | solution.py:67
  146.1 39.2 %all-gather.6.cloned.1.call-done = bf16[192,128,128]{2,1,0:T(8,128)(2,1)} async-done(((bf16[12,128,128]{2,1,0:T(8,128)(2,1)}), bf16[192,128,128]{2,1,0:T(8,128)(2,1)}) %all-gather.6.cloned.1.call-update) | async-done | bytes 6291472 | tf_op jit(solution)/shard_map/all_gather | solution.py:58
  185.3 7.2 %fusion.7 = bf16[16,16,128,128]{3,1,2,0:T(8,128)(2,1)S(1)} fusion(bf16[16,12,128,128]{3,2,1,0:T(8,128)(2,1)} %bitcast.66, s32[16,12]{1,0:T(8,128)S(1)} %eq.92), kind=kOutput, calls=%fused_computation.8 | convolution fusion | flops 104860672 | bytes 14680832 | tf_op jit(solution)/shard_map/gcs,gsab->gcab/dot_general | solution.py:43
  192.5 5.8 %copy.81 = bf16[16,4,4,128,128]{4,2,3,1,0:T(4,128)(2,1)} copy(bf16[16,4,4,128,128]{4,2,1,3,0:T(4,128)(2,1)S(1)} %bitcast.63) | data formatting | bytes 16777216 | tf_op jit(solution)/shard_map/reshape | solution.py:46
  198.4 13.1 %reshape.135 = bf16[16,512,512]{2,1,0:T(8,128)(2,1)} reshape(bf16[16,4,128,4,128]{4,3,2,1,0:T(4,128)(2,1)} %bitcast.64) | data formatting | bytes 16777216 | tf_op jit(solution)/shard_map/reshape | solution.py:47
  211.5 0.0 copy-start
  211.5 0.0 copy-start.1
  211.5 6.6 %convert_bitcast_fusion = bf16[16,128,512]{1,2,0:T(8,128)(2,1)S(1)} fusion(bf16[16,512,512]{2,1,0:T(8,128)(2,1)} %reshape.135, bf16[16,16,8,512]{3,2,1,0:T(8,128)(2,1)} %bitcast.75), kind=kOutput, calls=%fused_computation.16 | convolution fusion | flops 1074790400 | bytes 12582912 | tf_op jit(solution)/shard_map/tgr,grc->gtc/dot_general | solution.py:67
  218.0 0.6 convert_reduce_fusion
  218.6 0.7 multiply_convert_fusion
  219.3 0.0 all-gather.8.cloned.1.call-update
  219.3 0.0 reduce-scatter.2.cloned.1.call-start
  219.4 0.0 copy-done
  219.4 67.9 %all-gather.8.cloned.1.call-done = bf16[2048,512]{0,1:T(8,128)(2,1)} async-done(((bf16[128,512]{0,1:T(8,128)(2,1)}), bf16[2048,512]{0,1:T(8,128)(2,1)}) %all-gather.8.cloned.1.call-update) | async-done | bytes 2097168 | tf_op jit(solution)/shard_map/all_gather | solution.py:74
  287.3 0.2 mul.20
  287.5 0.0 copy-done.1
  287.5 4.2 %convolution_convert_fusion.2 = bf16[2048,512]{1,0:T(8,128)(2,1)} fusion(bf16[2048,512]{0,1:T(8,128)(2,1)} %all-gather.8.cloned.1.call-done, bf16[512,512]{1,0:T(8,128)(2,1)S(1)} %copy-done.1, bf16[64,8,4,128]{3,2,1,0:T(4,128)(2,1)S(1)} %bitcast.73), kind=kOutput, calls=%fused_computation.11 | convolution fusion | flops 1075052544 | bytes 5242880 | tf_op jit(solution)/shard_map/dot_general | solution.py:77
  291.7 0.0 reduce-scatter.2.cloned.1.call-update
  291.7 106.7 %reduce-scatter.2.cloned.1.call-done = bf16[64,512]{1,0:T(8,128)(2,1)} async-done(((bf16[2048,512]{1,0:T(8,128)(2,1)}), bf16[64,512]{1,0:T(8,128)(2,1)}) %reduce-scatter.2.cloned.1.call-update) | async-done | bytes 65552 | tf_op jit(solution)/shard_map/reduce_scatter | solution.py:76
  (5 shorter events, 0.1 us)
Async XLA Ops:
  6.5 94.2 %all-gather.4.cloned.1.call-start = ((), (), s32[]{:S(2)}) async-start(), calls=%async_computation.1 | async-start | bytes 6684672 | tf_op jit(solution)/shard_map/all_gather | solution.py:57
  10.8 174.5 %all-gather.6.cloned.1.call-start = ((), (), s32[]{:S(2)}) async-start(), calls=%async_computation.2 | async-start | bytes 6684672 | tf_op jit(solution)/shard_map/all_gather | solution.py:58
  15.2 272.1 %all-gather.8.cloned.1.call-start = ((), (), s32[]{:S(2)}) async-start(), calls=%async_computation.3 | async-start | bytes 2228224 | tf_op jit(solution)/shard_map/all_gather | solution.py:74
  211.5 7.9 %copy-start = (s32[4,4]{1,0:T(4,128)S(1)}, s32[4,4]{1,0:T(4,128)}, u32[]{:S(2)}) copy-start(s32[4,4]{1,0:T(4,128)} %param.13) | copy-start | bytes 196
  211.5 76.0 %copy-start.1 = (bf16[512,512]{1,0:T(8,128)(2,1)S(1)}, bf16[512,512]{1,0:T(8,128)(2,1)}, u32[]{:S(2)}) copy-start(bf16[512,512]{1,0:T(8,128)(2,1)} %param.10) | copy-start | bytes 1572868
  219.3 179.1 %reduce-scatter.2.cloned.1.call-start = ((), (), s32[]{:S(2)}) async-start(), calls=%async_computation.4 | async-start | bytes 2162688 | tf_op jit(solution)/shard_map/reduce_scatter | solution.py:76
Sparse Core Ops, SparseCore 0:
  11.0 89.7 all-gather.3
  102.8 82.4 all-gather.5
  219.5 67.7 all-gather.7
  291.9 106.5 reduce-scatter.1
where the time goes:
time: 407 us; the launch traced here: 405 us
  waiting for transfers between devices  273 us (67%)
  local copies, waits for them, and re-layouts  55.6 us (14%)
  matrix products  35.5 us (9%)
  blocking collectives  23.9 us (6%)
  between operations  13.9 us (3%)
    reduce_scatter x1, waiting for transfers between devices, on_device(): lax.psum_scatter(jnp.dot(all_hidden, down_eff, preferred_element_type=jnp...  107 us
    all_gather x1, waiting for transfers between devices, on_device(): all_hidden = lax.all_gather(hidden, 'row', axis=0, tiled=True)  67.9 us
    all_gather x1, waiting for transfers between devices, on_device(): gate_piece = lax.all_gather(gate_packed, 'row', axis=0, tiled=True)  58.8 us
    all_gather x1, waiting for transfers between devices, on_device(): up_piece = lax.all_gather(up_packed, 'row', axis=0, tiled=True)  39.2 us
    reshape x2, local copies, waits for them, and re-layouts, unpack_tiles(): return dense.reshape(groups, tile_rows * tile, tile_cols * tile)  26.3 us
    unnamed x1, blocking collectives  23.9 us
    dot_general x2, matrix products, unpack_tiles(): jnp.einsum('gcs,gsab->gcab', spread, packed, preferred_element_type=jnp.f...  17.6 us
    transpose x1, local copies, waits for them, and re-layouts, unpack_tiles(): dense.reshape(groups, tile_rows, tile_cols, tile, tile)  15.4 us
  transfers between devices with their start and end apart: 4, of which 4 were waited for; matrix products, arithmetic and copies ran while one was open for 13% of the time, Pallas kernels for 0%

commit v1 on v0

v1 whole, which is shorter than its diff:
```python
import functools

import jax
import jax.numpy as jnp
from jax import lax
from jax.experimental import pallas as pl
from jax.experimental.pallas import tpu as pltpu
from jax.sharding import PartitionSpec as P


def expand(weight, mask):
    rows, cols = weight.shape
    tile_rows, tile_cols = mask.shape
    tile = rows // tile_rows
    shaped = weight.reshape(tile_rows, tile, tile_cols, tile)
    return (shaped * mask.astype(weight.dtype)[:, None, :, None]).reshape(rows, cols)


def pack_tiles(weight, mask, slots):
    rows, cols = weight.shape
    tile_rows, tile_cols = mask.shape
    tile = rows // tile_rows
    count = tile_rows * tile_cols
    tiles = (
        weight.reshape(tile_rows, tile, tile_cols, tile)
        .transpose(0, 2, 1, 3)
        .reshape(count, tile * tile)
    )
    flags = mask.reshape(count)
    place = jnp.cumsum(flags) - 1
    chosen = (place[None, :] == jnp.arange(slots, dtype=jnp.int32)[:, None]) & (flags[None, :] == 1)
    packed = jnp.dot(chosen.astype(jnp.bfloat16), tiles, preferred_element_type=jnp.float32)
    packed = packed.astype(jnp.bfloat16).reshape(slots * tile, tile)
    where_from = jnp.sum(jnp.where(chosen, jnp.arange(count, dtype=jnp.int32)[None, :], 0), axis=1)
    return packed, where_from


def sparse_kernel(pos_ref, tok_ref, w_ref, out_ref, acc_g, acc_u, tot_g, tot_u, *, slots, tile, tile_cols):
    g = pl.program_id(0)

    @pl.when(g == 0)
    def _():
        tot_g[...] = jnp.zeros_like(tot_g)
        tot_u[...] = jnp.zeros_like(tot_u)

    acc_g[...] = jnp.zeros_like(acc_g)
    acc_u[...] = jnp.zeros_like(acc_u)
    base = g * (2 * slots)
    for which, acc in ((0, acc_g), (1, acc_u)):
        for s in range(slots):
            p = pos_ref[base + which * slots + s]
            i = p // tile_cols
            j = p % tile_cols
            t = tok_ref[:, pl.ds(pl.multiple_of(i * tile, tile), tile)]
            row0 = (which * slots + s) * tile
            w = w_ref[row0:row0 + tile, :]
            cols = pl.ds(pl.multiple_of(j * tile, tile), tile)
            acc[:, cols] += jnp.dot(t, w, preferred_element_type=jnp.float32)
    tot_g[...] += acc_g[...].astype(jnp.bfloat16).astype(jnp.float32)
    tot_u[...] += acc_u[...].astype(jnp.bfloat16).astype(jnp.float32)

    @pl.when(g == pl.num_programs(0) - 1)
    def _():
        v = tot_g[...]
        out_ref[...] = (v / (1.0 + jnp.exp(-v)) * tot_u[...]).astype(out_ref.dtype)


def sparse_hidden(pos, tokens, gathered, groups, slots, tile, tile_rows, tile_cols):
    tok_rows = tokens.shape[0]
    panel = tile_rows * tile
    width = tile_cols * tile
    block_rows = gathered.shape[1]
    kernel = functools.partial(sparse_kernel, slots=slots, tile=tile, tile_cols=tile_cols)
    grid_spec = pltpu.PrefetchScalarGridSpec(
        num_scalar_prefetch=1,
        grid=(groups,),
        in_specs=[
            pl.BlockSpec((tok_rows, panel), lambda g, pos: (0, g)),
            pl.BlockSpec((None, block_rows, tile), lambda g, pos: (g, 0, 0)),
        ],
        out_specs=pl.BlockSpec((tok_rows, width), lambda g, pos: (0, 0)),
        scratch_shapes=[pltpu.VMEM((tok_rows, width), jnp.float32) for _ in range(4)],
    )
    flops = 2 * 2 * groups * slots * tok_rows * tile * tile
    return pl.pallas_call(
        kernel,
        grid_spec=grid_spec,
        out_shape=jax.ShapeDtypeStruct((tok_rows, width), jnp.bfloat16),
        compiler_params=pltpu.CompilerParams(dimension_semantics=("arbitrary",)),
        cost_estimate=pl.CostEstimate(
            flops=flops, transcendentals=tok_rows * width,
            bytes_accessed=tokens.size * 2 + gathered.size * 2 + tok_rows * width * 2),
    )(pos, tokens, gathered)


def on_device(tokens, gate_weight, up_weight, down_weight, gate_mask, up_mask, down_mask):
    tile_rows, tile_cols = gate_mask.shape
    tile = gate_weight.shape[0] // tile_rows
    slots = 3 * tile_rows * tile_cols // 4
    groups = tokens.shape[1] // gate_weight.shape[0]
    gate_packed, gate_from = pack_tiles(gate_weight, gate_mask, slots)
    up_packed, up_from = pack_tiles(up_weight, up_mask, slots)
    where = jnp.concatenate([gate_from, up_from]).astype(jnp.bfloat16)
    where_rows = jnp.zeros((8, tile), jnp.bfloat16).at[0, : 2 * slots].set(where)
    combined = jnp.concatenate([gate_packed, up_packed, where_rows], axis=0)
    gathered = lax.all_gather(combined, "row", axis=0, tiled=False)
    pos = gathered[:, 2 * slots * tile, : 2 * slots].astype(jnp.int32).reshape(-1)
    hidden = sparse_hidden(pos, tokens, gathered, groups, slots, tile, tile_rows, tile_cols)
    all_hidden = lax.all_gather(hidden, "row", axis=0, tiled=True)
    down_eff = expand(down_weight, down_mask)
    return lax.psum_scatter(
        jnp.dot(all_hidden, down_eff, preferred_element_type=jnp.float32).astype(jnp.bfloat16),
        "col",
        scatter_dimension=0,
        tiled=True,
    )


def solution(mesh):
    return jax.shard_map(
        on_device,
        mesh=mesh,
        in_specs=(
            P("row", None),
            P("row", "col"),
            P("row", "col"),
            P("col", "row"),
            P("row", "col"),
            P("row", "col"),
            P("col", "row"),
        ),
        out_specs=P("col", "row"),
        check_vma=False,
    )
```

time: 407 us -> 366 us (0.90)
  local copies, waits for them, and re-layouts: 55.6 us -> 4.77 us
  waiting for transfers between devices: 273 us -> 322 us
  matrix products: 35.5 us -> 4.96 us
  blocking collectives: 23.9 us -> 0 us
  Pallas kernels: 0 us -> 16.2 us
    all_gather x2 -> x1, waiting for transfers between devices: 98 us -> 154 us  [on_device(): gathered = lax.all_gather(combined, 'row', axis=0, tiled=False)]
    reshape x5 -> x2, local copies, waits for them, and re-layouts: 33.7 us -> 0.66 us  [pack_tiles(): packed = packed.astype(jnp.bfloat16).reshape(slots * tile, tile)]
    dot_general x4 -> x0, matrix products: 30.5 us -> none  [the longest x2 17.6 us: unpack_tiles(): jnp.einsum('gcs,gsab->gcab', spread, packed, preferred_element_type=jnp.f...]
    unnamed x1 -> x0, blocking collectives: 23.9 us -> none
    pallas_call x0 -> x1, Pallas kernels: none -> 16.2 us  [sparse_hidden(): pl.pallas_call(kernel, grid_spec=grid_spec, out_shape=jax.ShapeDtypeStruc...]
    transpose x1 -> x0, local copies, waits for them, and re-layouts: 15.4 us -> none  [unpack_tiles(): dense.reshape(groups, tile_rows, tile_cols, tile, tile)]
    all_gather x1, waiting for transfers between devices: 67.9 us -> 62.1 us  [on_device(): all_hidden = lax.all_gather(hidden, 'row', axis=0, tiled=True)]
  transfers between devices with their start and end apart: 4 -> 3, of which waited for: 4 -> 3; matrix products, arithmetic and copies ran while one was open for 13% -> 0% of each run, Pallas kernels for 0% -> 0%
where the time goes in v1:
time: 366 us; the launch traced here: 365 us
  waiting for transfers between devices  322 us (88%)
  Pallas kernels  16.2 us (4%)
  between operations  13.2 us (4%)
  matrix products  4.96 us (1%)
  local copies, waits for them, and re-layouts  4.77 us (1%)
  other arithmetic  3.75 us (1%)
    all_gather x1, waiting for transfers between devices, on_device(): gathered = lax.all_gather(combined, 'row', axis=0, tiled=False)  154 us
    reduce_scatter x1, waiting for transfers between devices, on_device(): lax.psum_scatter(jnp.dot(all_hidden, down_eff, preferred_element_type=jnp...  106 us
    all_gather x1, waiting for transfers between devices, on_device(): all_hidden = lax.all_gather(hidden, 'row', axis=0, tiled=True)  62.1 us
    pallas_call x1, Pallas kernels, sparse_hidden(): pl.pallas_call(kernel, grid_spec=grid_spec, out_shape=jax.ShapeDtypeStruc...  16.2 us
  transfers between devices with their start and end apart: 3, of which 3 were waited for; matrix products, arithmetic and copies ran while one was open for 0% of the time, Pallas kernels for 0%

profile of v1, /device:TPU:1, one launch (start us, length us, event | category | flops | bytes accessed | tf_op | source)
XLA Modules:
  0.0 365.4 jit_solution(11515401112382616947)
XLA Ops:
  6.5 0.0 copy-start
  6.5 0.0 all-gather.6.cloned.1.call-start
  6.5 0.8 reshape.163
  7.4 0.7 broadcast_compare_fusion
  8.0 0.8 reshape.162
  8.8 0.7 broadcast_compare_fusion.1
  9.5 0.1 add_reduce_fusion
  9.6 0.1 eq.57
  9.8 0.1 add_reduce_fusion.1
  9.9 0.1 eq.52
  10.0 1.2 reshape.153
  11.1 0.1 copy.15
  11.2 0.1 select_reduce_fusion.1
  11.4 0.4 convolution_convert_fusion.1
  11.8 0.3 reshape.155
  12.1 0.0 copy-done
  12.1 0.1 reshape.157
  12.2 0.1 copy.17
  12.4 0.1 select_reduce_fusion
  12.5 0.4 convolution_convert_fusion
  12.9 0.3 reshape.159
  13.2 0.1 fusion.19
  13.3 1.0 pad_maximum_fusion
  14.3 0.0 all-gather.6.cloned.1.call-update
  14.3 0.0 all-gather.4.cloned.1.call-start
  14.4 153.8 %all-gather.6.cloned.1.call-done = bf16[49280,128]{1,0:T(8,128)(2,1)} async-done(((bf16[3080,128]{1,0:T(8,128)(2,1)}), bf16[49280,128]{1,0:T(8,128)(2,1)}) %all-gather.6.cloned.1.call-update) | async-done | bytes 12615696 | tf_op jit(solution)/shard_map/all_gather | solution.py:106
  168.2 0.8 fusion.5
  169.0 0.7 reshape.160.pos_ref
  169.6 0.0 copy-start.1
  169.6 0.0 copy-start.2
  169.6 16.2 %shard_map.73 = bf16[128,512]{1,0:T(8,128)(2,1)} custom-call(s32[384]{0:T(512)} %reshape.160.pos_ref, bf16[128,8192]{1,0:T(8,128)(2,1)} %tok_ref.1, bf16[16,3080,128]{2,1,0:T(8,128)(2,1)} %bitcast.24), custom_call_target="tpu_custom_call" | custom-call | flops 1610612736 | bytes 14843904 | tf_op jit(solution)/shard_map/pallas_call | solution.py:85
  185.9 0.0 all-gather.4.cloned.1.call-update
  185.9 0.0 reduce-scatter.2.cloned.1.call-start
  186.0 0.0 copy-done.1
  186.0 62.1 %all-gather.4.cloned.1.call-done = bf16[2048,512]{1,0:T(8,128)(2,1)} async-done(((bf16[128,512]{1,0:T(8,128)(2,1)}), bf16[2048,512]{1,0:T(8,128)(2,1)}) %all-gather.4.cloned.1.call-update) | async-done | bytes 2097168 | tf_op jit(solution)/shard_map/all_gather | solution.py:109
  248.0 0.2 mul.11
  248.2 0.0 copy-done.2
  248.3 4.2 %convolution_convert_fusion.2 = bf16[2048,512]{1,0:T(8,128)(2,1)} fusion(bf16[2048,512]{1,0:T(8,128)(2,1)} %all-gather.4.cloned.1.call-done, bf16[512,512]{1,0:T(8,128)(2,1)S(1)} %copy-done.2, bf16[64,8,4,128]{3,2,1,0:T(4,128)(2,1)S(1)} %bitcast.27), kind=kOutput, calls=%fused_computation.2 | convolution fusion | flops 1075052544 | bytes 5242880 | tf_op jit(solution)/shard_map/dot_general | solution.py:112
  252.4 0.0 reduce-scatter.2.cloned.1.call-update
  252.4 106.5 %reduce-scatter.2.cloned.1.call-done = bf16[64,512]{1,0:T(8,128)(2,1)} async-done(((bf16[2048,512]{1,0:T(8,128)(2,1)}), bf16[64,512]{1,0:T(8,128)(2,1)}) %reduce-scatter.2.cloned.1.call-update) | async-done | bytes 65552 | tf_op jit(solution)/shard_map/reduce_scatter | solution.py:111
  (4 shorter events, 0.1 us)
Async XLA Ops:
  6.5 5.6 %copy-start = (bf16[512,512]{1,0:T(8,128)(2,1)S(1)}, bf16[512,512]{1,0:T(8,128)(2,1)}, u32[]{:S(2)}) copy-start(bf16[512,512]{1,0:T(8,128)(2,1)} %param.11) | copy-start | bytes 1572868
  6.5 161.6 %all-gather.6.cloned.1.call-start = ((), (), s32[]{:S(2)}) async-start(), calls=%async_computation.3 | async-start | bytes 13404160 | tf_op jit(solution)/shard_map/all_gather | solution.py:106
  14.3 233.7 %all-gather.4.cloned.1.call-start = ((), (), s32[]{:S(2)}) async-start(), calls=%async_computation.1 | async-start | bytes 2228224 | tf_op jit(solution)/shard_map/all_gather | solution.py:109
  169.6 16.3 %copy-start.1 = (s32[4,4]{1,0:T(4,128)S(1)}, s32[4,4]{1,0:T(4,128)}, u32[]{:S(2)}) copy-start(s32[4,4]{1,0:T(4,128)} %param.15) | copy-start | bytes 196
  169.6 78.6 %copy-start.2 = (bf16[512,512]{1,0:T(8,128)(2,1)S(1)}, bf16[512,512]{1,0:T(8,128)(2,1)}, u32[]{:S(2)}) copy-start(bf16[512,512]{1,0:T(8,128)(2,1)} %param.12) | copy-start | bytes 1572868
  185.9 173.0 %reduce-scatter.2.cloned.1.call-start = ((), (), s32[]{:S(2)}) async-start(), calls=%async_computation.2 | async-start | bytes 2162688 | tf_op jit(solution)/shard_map/reduce_scatter | solution.py:111
Sparse Core Ops, SparseCore 0:
  14.4 153.7 all-gather.5
  186.0 61.9 all-gather.3
  252.6 106.2 reduce-scatter.1

commit v2 on v1

--- a/solution.py
+++ b/solution.py
@@ -108,12 +108,11 @@
     hidden = sparse_hidden(pos, tokens, gathered, groups, slots, tile, tile_rows, tile_cols)
     all_hidden = lax.all_gather(hidden, "row", axis=0, tiled=True)
     down_eff = expand(down_weight, down_mask)
-    return lax.psum_scatter(
-        jnp.dot(all_hidden, down_eff, preferred_element_type=jnp.float32).astype(jnp.bfloat16),
-        "col",
-        scatter_dimension=0,
-        tiled=True,
-    )
+    partial = jnp.dot(all_hidden, down_eff, preferred_element_type=jnp.float32).astype(jnp.bfloat16)
+    n_col = lax.axis_size("col")
+    pieces = lax.all_to_all(partial, "col", 0, 0, tiled=True)
+    pieces = pieces.reshape(n_col, pieces.shape[0] // n_col, pieces.shape[1])
+    return jnp.sum(pieces.astype(jnp.float32), axis=0).astype(jnp.bfloat16)
 
 
 def solution(mesh):

time: 366 us -> 304 us (0.83)
  waiting for transfers between devices: 322 us -> 216 us
  blocking collectives: 0 us -> 44.8 us
    reduce_scatter x1 -> x0, waiting for transfers between devices: 106 us -> none  [on_device(): lax.psum_scatter(jnp.dot(all_hidden, down_eff, preferred_element_type=jnp...]
    all_to_all x0 -> x1, blocking collectives: none -> 44.8 us  [on_device(): pieces = lax.all_to_all(partial, 'col', 0, 0, tiled=True)]
  transfers between devices with their start and end apart: 3 -> 2, of which waited for: 3 -> 2; matrix products, arithmetic and copies ran while one was open for 0% -> 0% of each run, Pallas kernels for 0% -> 0%
where the time goes in v2:
time: 304 us
  waiting for transfers between devices  216 us (71%)
  blocking collectives  44.8 us (15%)
  Pallas kernels  16.2 us (5%)
  between operations  13.5 us (4%)
  local copies, waits for them, and re-layouts  4.77 us (2%)
  other arithmetic  4.68 us (2%)
  matrix products  3.66 us (1%)
    all_gather x1, waiting for transfers between devices, on_device(): gathered = lax.all_gather(combined, 'row', axis=0, tiled=False)  154 us
    all_gather x1, waiting for transfers between devices, on_device(): all_hidden = lax.all_gather(hidden, 'row', axis=0, tiled=True)  62.1 us
    all_to_all x1, blocking collectives, on_device(): pieces = lax.all_to_all(partial, 'col', 0, 0, tiled=True)  44.8 us
    pallas_call x1, Pallas kernels, sparse_hidden(): pl.pallas_call(kernel, grid_spec=grid_spec, out_shape=jax.ShapeDtypeStruc...  16.2 us
  transfers between devices with their start and end apart: 2, of which 2 were waited for; matrix products, arithmetic and copies ran while one was open for 0% of the time, Pallas kernels for 0%

profile of v2, /device:TPU:1, one launch (start us, length us, event | category | flops | bytes accessed | tf_op | source)
XLA Modules:
  0.0 303.7 jit_solution(3986971165145324841)
XLA Ops:
  6.5 0.0 copy-start
  6.5 0.0 all-gather.6.cloned.1.call-start
  6.5 0.8 reshape.167
  7.4 0.7 broadcast_compare_fusion
  8.0 0.8 reshape.166
  8.8 0.7 broadcast_compare_fusion.1
  9.5 0.1 add_reduce_fusion
  9.6 0.1 eq.57
  9.8 0.1 add_reduce_fusion.1
  9.9 0.1 eq.52
  10.0 1.2 reshape.157
  11.1 0.1 copy.15
  11.2 0.1 select_reduce_fusion.1
  11.4 0.4 convolution_convert_fusion.1
  11.8 0.3 reshape.159
  12.1 0.0 copy-done
  12.1 0.1 reshape.161
  12.2 0.1 copy.17
  12.4 0.1 select_reduce_fusion
  12.5 0.4 convolution_convert_fusion
  12.9 0.3 reshape.163
  13.2 0.1 fusion.19
  13.3 1.0 pad_maximum_fusion
  14.3 0.0 all-gather.6.cloned.1.call-update
  14.3 0.0 all-gather.4.cloned.1.call-start
  14.4 153.8 %all-gather.6.cloned.1.call-done = bf16[49280,128]{1,0:T(8,128)(2,1)} async-done(((bf16[3080,128]{1,0:T(8,128)(2,1)}), bf16[49280,128]{1,0:T(8,128)(2,1)}) %all-gather.6.cloned.1.call-update) | async-done | bytes 12615696 | tf_op jit(solution)/shard_map/all_gather | solution.py:106
  168.2 0.8 fusion.5
  169.0 0.7 reshape.164.pos_ref
  169.6 0.0 copy-start.1
  169.6 0.0 copy-start.2
  169.6 16.2 %shard_map.73 = bf16[128,512]{1,0:T(8,128)(2,1)} custom-call(s32[384]{0:T(512)} %reshape.164.pos_ref, bf16[128,8192]{1,0:T(8,128)(2,1)} %tok_ref.1, bf16[16,3080,128]{2,1,0:T(8,128)(2,1)} %bitcast.25), custom_call_target="tpu_custom_call" | custom-call | flops 1610612736 | bytes 14843904 | tf_op jit(solution)/shard_map/pallas_call | solution.py:85
  185.9 0.0 all-gather.4.cloned.1.call-update
  185.9 0.0 copy-done.1
  185.9 62.1 %all-gather.4.cloned.1.call-done = bf16[2048,512]{1,0:T(8,128)(2,1)} async-done(((bf16[128,512]{1,0:T(8,128)(2,1)}), bf16[2048,512]{1,0:T(8,128)(2,1)}) %all-gather.4.cloned.1.call-update) | async-done | bytes 2097168 | tf_op jit(solution)/shard_map/all_gather | solution.py:109
  248.0 0.2 mul.11
  248.2 0.0 copy-done.2
  248.3 2.9 convolution_convert_fusion.2
  251.1 44.8 %all_to_all.9 = bf16[32,64,512]{2,1,0:T(8,128)(2,1)S(1)} all-to-all(bf16[32,64,512]{2,1,0:T(8,128)(2,1)S(1)} %bitcast.28), channel_id=1, replica_groups=mesh['row'=16,'col'=32] {'col'}, dimensions={0} | all-to-all | bytes 4194304 | tf_op jit(solution)/shard_map/all_to_all | solution.py:113
  295.9 0.9 reduce_sum.32
  (4 shorter events, 0.1 us)
Async XLA Ops:
  6.5 5.6 %copy-start = (bf16[512,512]{1,0:T(8,128)(2,1)S(1)}, bf16[512,512]{1,0:T(8,128)(2,1)}, u32[]{:S(2)}) copy-start(bf16[512,512]{1,0:T(8,128)(2,1)} %param.11) | copy-start | bytes 1572868
  6.5 161.6 %all-gather.6.cloned.1.call-start = ((), (), s32[]{:S(2)}) async-start(), calls=%async_computation.2 | async-start | bytes 13404160 | tf_op jit(solution)/shard_map/all_gather | solution.py:106
  14.3 233.7 %all-gather.4.cloned.1.call-start = ((), (), s32[]{:S(2)}) async-start(), calls=%async_computation.1 | async-start | bytes 2228224 | tf_op jit(solution)/shard_map/all_gather | solution.py:109
  169.6 16.3 %copy-start.1 = (s32[4,4]{1,0:T(4,128)S(1)}, s32[4,4]{1,0:T(4,128)}, u32[]{:S(2)}) copy-start(s32[4,4]{1,0:T(4,128)} %param.15) | copy-start | bytes 196
  169.6 78.6 %copy-start.2 = (bf16[512,512]{1,0:T(8,128)(2,1)S(1)}, bf16[512,512]{1,0:T(8,128)(2,1)}, u32[]{:S(2)}) copy-start(bf16[512,512]{1,0:T(8,128)(2,1)} %param.12) | copy-start | bytes 1572868
Sparse Core Ops, SparseCore 0:
  14.4 153.7 all-gather.5
  186.0 61.9 all-gather.3
